TPU v7x, 32 devices: a whole 2x2x4 slice. The times are simulated.
32 devices in a mesh: seq: 16 (over z, y, x), head: 2 (over core).
Axes of the slice: x: 2, y: 2, z: 4, core: 2. Of those that a mesh axis runs over, the one named last changes fastest.
Arguments:
- win_query: bfloat16 [4096, 4096], P('seq', 'head'), may hold values from -24 to 24
- win_key: bfloat16 [4096, 4096], P('seq', 'head'), may hold values from -24 to 24
- win_value: bfloat16 [4096, 4096], P('seq', 'head'), may hold values from -24 to 24
- clu_query: bfloat16 [4096, 4096], P('seq', 'head'), may hold values from -24 to 24
- clu_key: bfloat16 [4096, 4096], P('seq', 'head'), may hold values from -24 to 24
- clu_value: bfloat16 [4096, 4096], P('seq', 'head'), may hold values from -24 to 24
- cluster_ids: int32 [32, 4096], P('head', 'seq'), may hold values from 0 to 63, as said below
- win_gain: float32 [4096], P('head'), may hold values from 0.5 to 1.5
- clu_gain: float32 [4096], P('head'), may hold values from 0.5 to 1.5
- win_out_grad: bfloat16 [4096, 4096], P('seq', 'head'), may hold values from -9 to 9
- clu_out_grad: bfloat16 [4096, 4096], P('seq', 'head'), may hold values from -9 to 9
Outputs:
- win_normed: bfloat16 [4096, 4096], P('seq', 'head')
- clu_normed: bfloat16 [4096, 4096], P('seq', 'head')
- win_dq: bfloat16 [4096, 4096], P('seq', 'head')
- win_dk: bfloat16 [4096, 4096], P('seq', 'head')
- win_dv: bfloat16 [4096, 4096], P('seq', 'head')
- clu_dq: bfloat16 [4096, 4096], P('seq', 'head')
- clu_dk: bfloat16 [4096, 4096], P('seq', 'head')
- clu_dv: bfloat16 [4096, 4096], P('seq', 'head')
Inputs may be any that keep to these rules, and one draw needn't show every extreme that they name: `cluster_ids`: in every cluster head each cluster holds at most 8 of the tokens of each aligned block of 256 positions, hence at most 128 tokens in all; in every head one cluster holds exactly 8 tokens of every block.
All inputs are finite; a program needn't handle non-finite values.
Results may differ from a plain program's by a relative error of at most 0.035.
Values may be sent and summed in bfloat16 or wider, within the bound.
A program may use at most 192 MiB of HBM per device.

v0:
```python
import jax
import jax.numpy as jnp
from jax import lax
from jax.sharding import PartitionSpec as P

HW = 32
HC = 32
DH = 128
WINDOW = 256
SLOTS = 128
EPSILON = 1e-06


def from_behind(block, axis, distance):
    devices = range(lax.axis_size(axis))
    route = [(i - distance, i) for i in devices if i - distance in devices]
    return lax.ppermute(block, axis, route)


def split_heads(values):
    return values.reshape(values.shape[0], values.shape[1] // DH, DH)


def five_dims(values):
    return values.reshape(
        values.shape[0], values.shape[1], values.shape[2], values.shape[3] // DH, DH
    )


def softmax_rows(scores, allowed):
    masked = jnp.where(allowed, scores, -jnp.inf)
    top_row = jnp.max(masked, axis=-1, keepdims=True)
    summed = jnp.sum(jnp.exp(masked - top_row), axis=-1, keepdims=True)
    return jnp.exp(masked - (top_row + jnp.log(summed)))


def owner_attend(queries, key_rows, val_rows, filled, factor):
    layout = queries.shape
    sources, n_items, n_cap, n_heads = (layout[0], layout[1], layout[2], layout[3])
    member_count = sources * n_cap
    scores = jnp.einsum(
        "scahd,tcbhd->hcsatb", queries, key_rows, preferred_element_type=jnp.float32
    )
    scores = scores.reshape(n_heads, n_items, member_count, member_count) * factor
    live_cols = filled.transpose(3, 1, 0, 2).reshape(n_heads, n_items, 1, member_count) > 0
    row_pos = lax.broadcasted_iota(jnp.int32, (member_count, member_count), 0)
    col_pos = lax.broadcasted_iota(jnp.int32, (member_count, member_count), 1)
    allowed = live_cols & (col_pos <= row_pos) | (col_pos == row_pos)
    attn_prob = softmax_rows(scores, allowed)
    weights = attn_prob.astype(jnp.bfloat16)
    six_dims = (n_heads, n_items, sources, n_cap, sources, n_cap)
    outputs = jnp.einsum(
        "hcsatb,tcbhd->scahd",
        weights.reshape(six_dims),
        val_rows,
        preferred_element_type=jnp.float32,
    ).astype(jnp.bfloat16)
    return (attn_prob, weights, outputs)


def owner_gradients(queries, key_rows, val_rows, attn_prob, weights, outputs, grad_rows, factor):
    layout = queries.shape
    sources, n_items, n_cap, n_heads = (layout[0], layout[1], layout[2], layout[3])
    member_count = sources * n_cap
    six_dims = (n_heads, n_items, sources, n_cap, sources, n_cap)
    flat_dims = (sources, n_items, n_cap, n_heads * DH)
    row_dot = jnp.sum(grad_rows.astype(jnp.float32) * outputs.astype(jnp.float32), axis=-1)
    row_dot = row_dot.transpose(3, 1, 0, 2).reshape(n_heads, n_items, member_count, 1)
    slope_rows = jnp.einsum(
        "scahd,tcbhd->hcsatb", grad_rows, val_rows, preferred_element_type=jnp.float32
    )
    slope_rows = slope_rows.reshape(n_heads, n_items, member_count, member_count)
    change = (attn_prob * (slope_rows - row_dot)).astype(jnp.bfloat16).reshape(six_dims)
    grad_q = jnp.einsum("hcsatb,tcbhd->scahd", change, key_rows, preferred_element_type=jnp.float32)
    grad_k = jnp.einsum("hcsatb,scahd->tcbhd", change, queries, preferred_element_type=jnp.float32)
    grad_v = jnp.einsum(
        "hcsatb,scahd->tcbhd",
        weights.reshape(six_dims),
        grad_rows,
        preferred_element_type=jnp.float32,
    )
    grad_q = (grad_q * factor).astype(jnp.bfloat16).reshape(flat_dims)
    grad_k = (grad_k * factor).astype(jnp.bfloat16).reshape(flat_dims)
    grad_v = grad_v.astype(jnp.bfloat16).reshape(flat_dims)
    return (grad_q, grad_k, grad_v)


def body(
    win_query,
    win_key,
    win_value,
    clu_query,
    clu_key,
    clu_value,
    cluster_ids,
    win_gain,
    clu_gain,
    win_out_grad,
    clu_out_grad,
):
    n_rows = win_query.shape[0]
    factor = DH ** (-0.5)
    feat_width = (HW + HC) * DH
    sources = lax.axis_size("seq")
    position = lax.axis_index("seq")
    n_cap = SLOTS // sources
    owned_count = 2 * n_rows // SLOTS
    pool_size = 2 * n_rows
    clu_heads = clu_query.shape[1] // DH
    rim_rows = jnp.stack([win_key, win_value])
    before = from_behind(rim_rows, "seq", 1)
    key_local = split_heads(jnp.concatenate([before[0], win_key], axis=0))
    val_local = split_heads(jnp.concatenate([before[1], win_value], axis=0))
    query_win = split_heads(win_query)
    row_pos = lax.broadcasted_iota(jnp.int32, (n_rows, n_rows + WINDOW), 0)
    col_pos = lax.broadcasted_iota(jnp.int32, (n_rows, n_rows + WINDOW), 1)
    gap_pos = row_pos + WINDOW - col_pos
    allowed = (gap_pos >= 0) & (gap_pos < WINDOW) & ((col_pos >= WINDOW) | (position > 0))
    scores = (
        jnp.einsum("ihd,jhd->hij", query_win, key_local, preferred_element_type=jnp.float32)
        * factor
    )
    prob_win = softmax_rows(scores, allowed)
    weight_win = prob_win.astype(jnp.bfloat16)
    attn_win = jnp.einsum(
        "hij,jhd->ihd", weight_win, val_local, preferred_element_type=jnp.float32
    ).astype(jnp.bfloat16)
    row_ids = lax.broadcasted_iota(jnp.int32, (n_rows, n_rows), 0)
    col_ids = lax.broadcasted_iota(jnp.int32, (n_rows, n_rows), 1)
    same_cluster = (cluster_ids[:, :, None] == cluster_ids[:, None, :]) & (col_ids < row_ids)
    rank_in = jnp.sum(same_cluster.astype(jnp.int32), axis=-1)
    slot_at = cluster_ids * n_cap + rank_in
    picker = (
        lax.broadcasted_iota(jnp.int32, (clu_heads, pool_size, n_rows), 1) == slot_at[:, None, :]
    ).astype(jnp.bfloat16)

    def dispatch(values):
        spread = jnp.einsum(
            "hpt,thd->phd", picker, split_heads(values), preferred_element_type=jnp.float32
        )
        return spread.astype(jnp.bfloat16).reshape(sources, owned_count, n_cap, clu_heads * DH)

    def collect(values):
        merged = jnp.einsum(
            "hpt,phd->thd",
            picker,
            values.reshape(pool_size, clu_heads, DH),
            preferred_element_type=jnp.float32,
        )
        return merged.astype(jnp.bfloat16).reshape(n_rows, clu_heads * DH)

    filled = jnp.sum(picker, axis=2).transpose(1, 0).reshape(sources, owned_count, n_cap, clu_heads)
    sent_query = dispatch(clu_query)
    sent_key = dispatch(clu_key)
    sent_value = dispatch(clu_value)
    queries = lax.all_to_all(sent_query, "seq", split_axis=0, concat_axis=0, tiled=True)
    key_rows = lax.all_to_all(sent_key, "seq", split_axis=0, concat_axis=0, tiled=True)
    val_rows = lax.all_to_all(sent_value, "seq", split_axis=0, concat_axis=0, tiled=True)
    live_rows = lax.all_to_all(filled, "seq", split_axis=0, concat_axis=0, tiled=True)
    q_five = five_dims(queries)
    k_five = five_dims(key_rows)
    v_five = five_dims(val_rows)
    attn_prob, weights, outputs = owner_attend(q_five, k_five, v_five, live_rows, factor)
    returned = lax.all_to_all(
        outputs.reshape(queries.shape), "seq", split_axis=0, concat_axis=0, tiled=True
    )
    result = (returned, q_five, k_five, v_five, attn_prob, weights, outputs)
    returned = result[0]
    attn_clu = collect(returned)
    flat_win = attn_win.reshape(n_rows, -1).astype(jnp.float32)
    flat_clu = attn_clu.astype(jnp.float32)
    sq_total = lax.psum(
        jnp.sum(flat_win * flat_win, axis=1) + jnp.sum(flat_clu * flat_clu, axis=1), "head"
    )
    inv_rms = 1.0 / jnp.sqrt(sq_total / feat_width + EPSILON)
    win_normed = (flat_win * inv_rms[:, None] * win_gain).astype(jnp.bfloat16)
    clu_normed = (flat_clu * inv_rms[:, None] * clu_gain).astype(jnp.bfloat16)
    grad_win = win_out_grad.astype(jnp.float32) * win_gain
    grad_clu = clu_out_grad.astype(jnp.float32) * clu_gain
    dot_total = lax.psum(
        jnp.sum(grad_win * flat_win, axis=1) + jnp.sum(grad_clu * flat_clu, axis=1), "head"
    )
    coef_rows = inv_rms**3 * dot_total / feat_width
    dout_win = (inv_rms[:, None] * grad_win - coef_rows[:, None] * flat_win).astype(jnp.bfloat16)
    dout_clu = (inv_rms[:, None] * grad_clu - coef_rows[:, None] * flat_clu).astype(jnp.bfloat16)
    dout_heads = split_heads(dout_win)
    row_dot_win = jnp.sum(dout_heads.astype(jnp.float32) * attn_win.astype(jnp.float32), axis=-1)
    slope_win = jnp.einsum(
        "ihd,jhd->hij", dout_heads, val_local, preferred_element_type=jnp.float32
    )
    change_win = (prob_win * (slope_win - row_dot_win.T[:, :, None])).astype(jnp.bfloat16)
    win_dq = jnp.einsum("hij,jhd->ihd", change_win, key_local, preferred_element_type=jnp.float32)
    win_dq = (win_dq * factor).astype(jnp.bfloat16).reshape(n_rows, -1)
    key_terms = jnp.einsum(
        "hij,ihd->jhd", change_win, query_win, preferred_element_type=jnp.float32
    )
    val_terms = jnp.einsum(
        "hij,ihd->jhd", weight_win, dout_heads, preferred_element_type=jnp.float32
    )
    rim_terms = jnp.stack([key_terms[:WINDOW], val_terms[:WINDOW]]).reshape(2, WINDOW, -1)
    after_rim = from_behind(rim_terms.astype(jnp.bfloat16), "seq", -1).astype(rim_terms.dtype)
    win_dk = key_terms[WINDOW:].reshape(n_rows, -1).at[n_rows - WINDOW :].add(after_rim[0])
    win_dk = (win_dk * factor).astype(jnp.bfloat16)
    win_dv = (
        val_terms[WINDOW:]
        .reshape(n_rows, -1)
        .at[n_rows - WINDOW :]
        .add(after_rim[1])
        .astype(jnp.bfloat16)
    )
    grad_sent = dispatch(dout_clu)
    grad_owned = lax.all_to_all(grad_sent, "seq", split_axis=0, concat_axis=0, tiled=True)
    grad_q, grad_k, grad_v = owner_gradients(
        result[1],
        result[2],
        result[3],
        result[4],
        result[5],
        result[6],
        five_dims(grad_owned),
        factor,
    )
    home_rows = (
        lax.all_to_all(grad_q, "seq", split_axis=0, concat_axis=0, tiled=True),
        lax.all_to_all(grad_k, "seq", split_axis=0, concat_axis=0, tiled=True),
        lax.all_to_all(grad_v, "seq", split_axis=0, concat_axis=0, tiled=True),
    )
    clu_dq = collect(home_rows[0])
    clu_dk = collect(home_rows[1])
    clu_dv = collect(home_rows[2])
    return (win_normed, clu_normed, win_dq, win_dk, win_dv, clu_dq, clu_dk, clu_dv)


def solution(mesh):
    return jax.shard_map(
        body,
        mesh=mesh,
        in_specs=(
            P("seq", "head"),
            P("seq", "head"),
            P("seq", "head"),
            P("seq", "head"),
            P("seq", "head"),
            P("seq", "head"),
            P("head", "seq"),
            P("head"),
            P("head"),
            P("seq", "head"),
            P("seq", "head"),
        ),
        out_specs=(
            P("seq", "head"),
            P("seq", "head"),
            P("seq", "head"),
            P("seq", "head"),
            P("seq", "head"),
            P("seq", "head"),
            P("seq", "head"),
            P("seq", "head"),
        ),
        check_vma=False,
    )
```

profile of v0, /device:TPU:14, one launch (start us, length us, event | category | flops | bytes accessed | tf_op | source)
XLA Modules:
  0.0 635.6 jit_solution(10428212256974955099)
XLA Ops:
  0.7 2.1 convert_reduce_fusion
  5.6 7.1 %all-to-all-start.1 = ((bf16[16,2,256]{2,1,0:T(2,128)(2,1)}), bf16[16,2,256]{2,1,0:T(2,128)(2,1)S(1)}, u32[]{:S(2)}, u32[]{:S(2)}) async-start(bf16[16,2,256]{2,1,0:T(2,128)(2,1)} %reshape.323), calls=%async_computation.1 | async-start | bytes 32768 | tf_op jit(solution)/shard_map/all_to_all | solution.py:159
  15.7 2.3 reshape.287
  18.0 7.0 %all-to-all-start.3 = ((bf16[16,4,8,2048]{3,2,1,0:T(8,128)(2,1)}), bf16[16,4,8,2048]{3,2,1,0:T(8,128)(2,1)S(1)}, u32[]{:S(2)}, u32[]{:S(2)}) async-start(bf16[16,4,8,2048]{3,2,1,0:T(8,128)(2,1)} %reshape.287), calls=%async_computation.3 | async-start | bytes 4194304 | tf_op jit(solution)/shard_map/all_to_all | solution.py:157
  26.6 2.7 copy.199
  29.3 4.2 reshape.284
  33.5 39.0 %all-to-all-done.3 = bf16[16,4,8,2048]{3,2,1,0:T(8,128)(2,1)S(1)} async-done(((bf16[16,4,8,2048]{3,2,1,0:T(8,128)(2,1)}), bf16[16,4,8,2048]{3,2,1,0:T(8,128)(2,1)S(1)}, u32[]{:S(2)}, u32[]{:S(2)}) %all-to-all-start.3) | async-done | bytes 2097184 | tf_op jit(solution)/shard_map/all_to_all | solution.py:157
  72.5 5.4 all-to-all-start.2
  79.5 2.7 copy.194
  82.2 4.2 reshape.280
  86.4 38.7 %all-to-all-done.2 = bf16[16,4,8,2048]{3,2,1,0:T(8,128)(2,1)} async-done(((bf16[16,4,8,2048]{3,2,1,0:T(8,128)(2,1)}), bf16[16,4,8,2048]{3,2,1,0:T(8,128)(2,1)}, u32[]{:S(2)}, u32[]{:S(2)}) %all-to-all-start.2) | async-done | bytes 2097184 | tf_op jit(solution)/shard_map/all_to_all | solution.py:156
  125.1 5.1 all-to-all-start
  131.7 2.3 copy.186
  134.0 2.7 pad_maximum_fusion
  136.7 3.4 collective-permute-start
  143.5 3.5 copy.291
  147.0 30.7 %all-to-all-done = bf16[16,4,8,2048]{3,2,1,0:T(8,128)(2,1)} async-done(((bf16[16,4,8,2048]{3,2,1,0:T(8,128)(2,1)}), bf16[16,4,8,2048]{3,2,1,0:T(8,128)(2,1)}, u32[]{:S(2)}, u32[]{:S(2)}) %all-to-all-start) | async-done | bytes 2097184 | tf_op jit(solution)/shard_map/all_to_all | solution.py:158
  177.7 2.2 copy.290
  180.0 21.8 %fusion.119 = (f32[16,4,16,8]{3,2,1,0:T(8,128)}, f32[16,4,16,8,16,8]{4,3,5,2,1,0:T(8,128)}) fusion(bf16[16,4,8,16,128,1]{4,3,2,1,0,5:T(8,128)(2,1)} %bitcast.229, bf16[16,4,8,16,128,1]{4,3,2,1,0,5:T(8,128)(2,1)} %bitcast.215, pred[16,8,16,8]{2,1,3,0:T(8,128)(4,1)S(1)} %copy-done.28, pred[16,8,16,8]{2,1,3,0:T(8,128)(4,1)S(1)} %get-tuple-element.92, ...), kind=kOutput, calls=%fused_computation.139 | convolution fusion | flops 273670144 | bytes 8462336 | tf_op jit(solution)/shard_map/scahd,tcbhd->hcsatb/dot_general | solution.py:41
  201.8 16.3 %exponential_reduce_fusion = f32[16,4,16,8]{3,2,1,0:T(8,128)S(1)} fusion(f32[16,4,16,8,16,8]{4,3,5,2,1,0:T(8,128)} %get-tuple-element.99, f32[16,4,16,8]{3,2,1,0:T(8,128)} %get-tuple-element.98), kind=kLoop, calls=%fused_computation.2 | loop fusion | flops 2088960 | bytes 4259840 | tf_op jit(solution)/shard_map/reduce_sum | solution.py:33
  218.2 4.2 copy-done.2
  222.3 8.6 %fusion = bf16[16,4,16,8,16,8]{4,3,5,2,1,0:T(8,128)(2,1)} fusion(f32[16,4,16,8,16,8]{4,3,5,2,1,0:T(8,128)S(1)} %copy-done.2, f32[16,4,16,8]{3,2,1,0:T(8,128)S(1)} %log_add_fusion), kind=kLoop, calls=%fused_computation.4 | loop fusion | flops 2097152 | bytes 6324224 | tf_op jit(solution)/shard_map/convert_element_type | solution.py:50
  230.9 20.6 %fusion.63 = bf16[16,4,8,16,128]{4,0,2,3,1:T(8,128)(2,1)S(1)} fusion(bf16[16,4,16,8,16,8]{4,3,5,2,1,0:T(8,128)(2,1)} %fusion, bf16[16,4,8,16,128,1]{4,3,2,1,0,5:T(8,128)(2,1)S(1)} %bitcast.209), kind=kOutput, calls=%fused_computation.92 | convolution fusion | flops 269484032 | bytes 6291456 | tf_op jit(solution)/shard_map/hcsatb,tcbhd->scahd/dot_general | solution.py:52
  254.2 2.3 reshape.289
  256.5 10.3 %all-to-all-start.4 = ((bf16[16,4,8,2048]{3,2,1,0:T(8,128)(2,1)}), bf16[16,4,8,2048]{3,2,1,0:T(8,128)(2,1)}, u32[]{:S(2)}, u32[]{:S(2)}) async-start(bf16[16,4,8,2048]{3,2,1,0:T(8,128)(2,1)} %reshape.289), calls=%async_computation.4 | async-start | bytes 4194304 | tf_op jit(solution)/shard_map/all_to_all | solution.py:164
  268.8 2.8 fusion.118
  272.9 2.5 fusion.19
  279.0 3.5 fusion.53
  284.4 27.7 %all-to-all-done.4 = bf16[16,4,8,2048]{3,2,1,0:T(8,128)(2,1)} async-done(((bf16[16,4,8,2048]{3,2,1,0:T(8,128)(2,1)}), bf16[16,4,8,2048]{3,2,1,0:T(8,128)(2,1)}, u32[]{:S(2)}, u32[]{:S(2)}) %all-to-all-start.4) | async-done | bytes 2097184 | tf_op jit(solution)/shard_map/all_to_all | solution.py:164
  312.1 2.2 copy.293
  314.3 3.4 multiply_reduce_fusion.3
  317.7 3.0 copy.209
  320.8 2.5 multiply_reduce_fusion.1
  323.3 2.5 all-reduce
  325.8 5.1 subtract_convert_fusion
  331.5 3.3 convert_bitcast_fusion
  334.8 3.4 copy.228
  338.2 2.3 reshape.298
  340.5 52.9 %all_to_all.45 = bf16[16,4,8,2048]{3,2,1,0:T(8,128)(2,1)S(1)} all-to-all(bf16[16,4,8,2048]{3,2,1,0:T(8,128)(2,1)} %reshape.298), channel_id=1, replica_groups=mesh['seq'=16,'head'=2] {'seq'}, dimensions={0} | all-to-all | bytes 4194304 | tf_op jit(solution)/shard_map/all_to_all | solution.py:212
  396.3 8.1 %fusion.73 = bf16[16,4,8,16,128]{4,0,2,3,1:T(8,128)(2,1)S(1)} fusion(bf16[16,4,16,8,16,8]{4,3,5,2,1,0:T(8,128)(2,1)} %fusion, bf16[16,4,8,16,128,1]{4,3,2,1,0,5:T(8,128)(2,1)S(1)} %bitcast.204), kind=kOutput, calls=%fused_computation.94 | convolution fusion | flops 269484032 | bytes 6291456 | tf_op jit(solution)/shard_map/hcsatb,scahd->tcbhd/dot_general | solution.py:76
  404.4 2.7 copy.243
  407.2 4.2 reshape.306
  411.3 6.8 %all-to-all-start.8 = ((bf16[16,4,8,2048]{3,2,1,0:T(8,128)(2,1)}), bf16[16,4,8,2048]{3,2,1,0:T(8,128)(2,1)}, u32[]{:S(2)}, u32[]{:S(2)}) async-start(bf16[16,4,8,2048]{3,2,1,0:T(8,128)(2,1)} %reshape.306), calls=%async_computation.8 | async-start | bytes 4194304 | tf_op jit(solution)/shard_map/all_to_all | solution.py:226
  418.4 29.2 %multiply_convert_fusion = bf16[16,4,16,8,16,8]{4,3,5,2,1,0:T(8,128)(2,1)} fusion(f32[16,4,16,8,16,8]{4,3,5,2,1,0:T(8,128)} %get-tuple-element.99, f32[16,4,16,8]{3,2,1,0:T(8,128)S(1)} %copy.232, f32[16,4,16,8]{3,2,1,0:T(8,128)S(1)} %copy-done.13, bf16[16,4,8,16,128,1]{4,3,2,1,0,5:T(8,128)(2,1)} %bitcast.210, bf16[16,4,8,16,128,1]{4,3,2,1,0,5:T(8,128)(2,1)S(1)} %bitcast.205), kind=kOutput, calls=%fused_computation | convolution fusion | flops 272629760 | bytes 10551296 | tf_op jit(solution)/shard_map/scahd,tcbhd->hcsatb/dot_general | solution.py:69
  447.6 8.1 %fusion.68 = bf16[16,4,8,16,128]{4,0,2,3,1:T(8,128)(2,1)S(1)} fusion(bf16[16,4,16,8,16,8]{4,3,5,2,1,0:T(8,128)(2,1)} %multiply_convert_fusion, bf16[16,4,8,16,128,1]{4,3,2,1,0,5:T(8,128)(2,1)S(1)} %bitcast.216), kind=kOutput, calls=%fused_computation.93 | convolution fusion | flops 270532608 | bytes 6291456 | tf_op jit(solution)/shard_map/hcsatb,scahd->tcbhd/dot_general | solution.py:75
  457.1 2.3 reshape.303
  459.4 5.6 all-to-all-done.8
  465.0 5.1 all-to-all-start.7
  472.3 7.8 %convolution_bitcast_fusion = f32[512,16,128]{0,2,1:T(8,128)} fusion(bf16[256,16,128]{0,2,1:T(8,128)(2,1)S(1)} %bitcast.213, f32[16,512,256]{2,1,0:T(8,128)} %copy-done.3, f32[16,256]{1,0:T(8,128)S(1)} %log_add_fusion.1, pred[256,512]{0,1:T(8,128)(4,1)S(1)} %fusion.104), kind=kOutput, calls=%fused_computation.46 | convolution fusion | flops 545259520 | bytes 13778944 | tf_op jit(solution)/shard_map/hij,ihd->jhd/dot_general | solution.py:197
  480.1 4.3 multiply_convert_fusion.1
  484.5 20.9 %fusion.58 = bf16[16,4,8,16,128]{4,0,2,3,1:T(8,128)(2,1)S(1)} fusion(bf16[16,4,16,8,16,8]{4,3,5,2,1,0:T(8,128)(2,1)} %multiply_convert_fusion, bf16[16,4,8,16,128,1]{4,3,2,1,0,5:T(8,128)(2,1)S(1)} %bitcast.230), kind=kOutput, calls=%fused_computation.91 | convolution fusion | flops 270532608 | bytes 6291456 | tf_op jit(solution)/shard_map/hcsatb,tcbhd->scahd/dot_general | solution.py:74
  506.8 2.4 reshape.300
  509.1 8.3 %all-to-all-done.7 = bf16[16,4,8,2048]{3,2,1,0:T(8,128)(2,1)} async-done(((bf16[16,4,8,2048]{3,2,1,0:T(8,128)(2,1)}), bf16[16,4,8,2048]{3,2,1,0:T(8,128)(2,1)}, u32[]{:S(2)}, u32[]{:S(2)}) %all-to-all-start.7) | async-done | bytes 2097184 | tf_op jit(solution)/shard_map/all_to_all | solution.py:225
  517.5 5.4 all-to-all-start.6
  522.9 3.7 convolution_bitcast_fusion.1
  533.3 2.7 collective-permute-start.1
  540.8 2.4 copy.245
  547.0 66.9 %collective-permute-done.1 = bf16[2,256,2048]{2,1,0:T(8,128)(2,1)} collective-permute-done((bf16[2,256,2048]{2,1,0:T(8,128)(2,1)}, bf16[2,256,2048]{2,1,0:T(8,128)(2,1)}, u32[]{:S(2)}, u32[]{:S(2)}) %collective-permute-start.1) | collective-permute-done | bytes 2097184 | tf_op jit(solution)/shard_map/ppermute | solution.py:17
  613.9 2.1 convert_element_type.197
  616.1 2.2 fusion.40
  618.3 2.2 copy.297
  624.0 2.2 copy.296
  626.2 2.1 fusion.87
  629.7 2.2 copy.295
  (132 shorter events, 57.6 us)
Async XLA Ops:
  0.6 12.1 %copy-start = (bf16[256,2048]{1,0:T(8,128)(2,1)S(1)}, bf16[256,2048]{1,0:T(8,128)(2,1)}, u32[]{:S(2)}) copy-start(bf16[256,2048]{1,0:T(8,128)(2,1)} %param.23) | copy-start | bytes 3145732
  3.6 328.0 %copy-start.29 = (s32[16,256]{1,0:T(8,128)}, s32[16,256]{1,0:T(8,128)S(1)}, u32[]{:S(2)}) copy-start(s32[16,256]{1,0:T(8,128)S(1)} %multiply_add_fusion) | copy-start | bytes 49156
  5.6 12.4 %all-to-all-start.1 = ((bf16[16,2,256]{2,1,0:T(2,128)(2,1)}), bf16[16,2,256]{2,1,0:T(2,128)(2,1)S(1)}, u32[]{:S(2)}, u32[]{:S(2)}) async-start(bf16[16,2,256]{2,1,0:T(2,128)(2,1)} %reshape.323), calls=%async_computation.1 | async-start | bytes 32768 | tf_op jit(solution)/shard_map/all_to_all | solution.py:159
  18.0 7.1 %copy-start.33 = (bf16[256,2048]{1,0:T(8,128)(2,1)S(1)}, bf16[256,2048]{1,0:T(8,128)(2,1)}, u32[]{:S(2)}) copy-start(bf16[256,2048]{1,0:T(8,128)(2,1)} %param.22) | copy-start | bytes 3145732
  18.0 54.5 %all-to-all-start.3 = ((bf16[16,4,8,2048]{3,2,1,0:T(8,128)(2,1)}), bf16[16,4,8,2048]{3,2,1,0:T(8,128)(2,1)S(1)}, u32[]{:S(2)}, u32[]{:S(2)}) async-start(bf16[16,4,8,2048]{3,2,1,0:T(8,128)(2,1)} %reshape.287), calls=%async_computation.3 | async-start | bytes 4194304 | tf_op jit(solution)/shard_map/all_to_all | solution.py:157
  33.5 44.4 %copy-start.34 = (bf16[256,2048]{1,0:T(8,128)(2,1)S(1)}, bf16[256,2048]{1,0:T(8,128)(2,1)}, u32[]{:S(2)}) copy-start(bf16[256,2048]{1,0:T(8,128)(2,1)} %param.24) | copy-start | bytes 3145732
  72.5 52.6 %all-to-all-start.2 = ((bf16[16,4,8,2048]{3,2,1,0:T(8,128)(2,1)}), bf16[16,4,8,2048]{3,2,1,0:T(8,128)(2,1)}, u32[]{:S(2)}, u32[]{:S(2)}) async-start(bf16[16,4,8,2048]{3,2,1,0:T(8,128)(2,1)} %reshape.284), calls=%async_computation.2 | async-start | bytes 4194304 | tf_op jit(solution)/shard_map/all_to_all | solution.py:156
  125.1 52.6 %all-to-all-start = ((bf16[16,4,8,2048]{3,2,1,0:T(8,128)(2,1)}), bf16[16,4,8,2048]{3,2,1,0:T(8,128)(2,1)}, u32[]{:S(2)}, u32[]{:S(2)}) async-start(bf16[16,4,8,2048]{3,2,1,0:T(8,128)(2,1)} %reshape.280), calls=%async_computation | async-start | bytes 4194304 | tf_op jit(solution)/shard_map/all_to_all | solution.py:158
  136.7 132.1 %collective-permute-start = (bf16[2,256,2048]{1,2,0:T(8,128)(2,1)}, bf16[2,256,2048]{1,2,0:T(8,128)(2,1)}, u32[]{:S(2)}, u32[]{:S(2)}) collective-permute-start(bf16[2,256,2048]{1,2,0:T(8,128)(2,1)} %pad_maximum_fusion), channel_id=1, source_target_pairs={{0,2},{2,4},{4,6},{6,8},{8,10},{10,12},{12,14},{14,16},{16,18},{18... | collective-permute-start | bytes 6291464 | tf_op jit(solution)/shard_map/ppermute | solution.py:17
  177.7 2.3 copy-start.28
  179.9 51.0 %copy-start.6 = (bf16[64,8,16,128]{3,2,1,0:T(8,128)(2,1)}, bf16[64,8,16,128]{3,2,1,0:T(8,128)(2,1)S(1)}, u32[]{:S(2)}) copy-start(bf16[64,8,16,128]{3,2,1,0:T(8,128)(2,1)S(1)} %copy.290) | copy-start | bytes 6291460
  201.8 16.3 %copy-start.20 = (f32[16,4,16,8]{3,2,1,0:T(8,128)S(1)}, f32[16,4,16,8]{3,2,1,0:T(8,128)}, u32[]{:S(2)}) copy-start(f32[16,4,16,8]{3,2,1,0:T(8,128)} %get-tuple-element.98) | copy-start | bytes 98308
  201.8 20.6 %copy-start.2 = (f32[16,4,16,8,16,8]{4,3,5,2,1,0:T(8,128)S(1)}, f32[16,4,16,8,16,8]{4,3,5,2,1,0:T(8,128)}, u32[]{:S(2)}) copy-start(f32[16,4,16,8,16,8]{4,3,5,2,1,0:T(8,128)} %get-tuple-element.99) | copy-start | bytes 12582916
  222.3 8.6 %copy-start.12 = (f32[16,4,16,8]{3,2,1,0:T(8,128)}, f32[16,4,16,8]{3,2,1,0:T(8,128)S(1)}, u32[]{:S(2)}) copy-start(f32[16,4,16,8]{3,2,1,0:T(8,128)S(1)} %log_add_fusion) | copy-start | bytes 98308
  251.5 1.4 copy-start.9
  256.5 55.6 %all-to-all-start.4 = ((bf16[16,4,8,2048]{3,2,1,0:T(8,128)(2,1)}), bf16[16,4,8,2048]{3,2,1,0:T(8,128)(2,1)}, u32[]{:S(2)}, u32[]{:S(2)}) async-start(bf16[16,4,8,2048]{3,2,1,0:T(8,128)(2,1)} %reshape.289), calls=%async_computation.4 | async-start | bytes 4194304 | tf_op jit(solution)/shard_map/all_to_all | solution.py:164
  266.8 1.2 copy-start.22
  268.1 4.9 copy-start.23
  268.6 4.3 copy-start.14
  275.4 3.5 copy-start.3
  275.4 3.5 copy-start.18
  275.5 3.5 copy-start.26
  317.7 3.0 copy-start.17
  317.7 3.0 copy-start.31
  317.7 3.0 copy-start.32
  393.4 1.6 copy-start.10
  411.3 7.1 %copy-start.13 = (f32[16,4,16,8]{3,2,1,0:T(8,128)S(1)}, f32[16,4,16,8]{3,2,1,0:T(8,128)}, u32[]{:S(2)}) copy-start(f32[16,4,16,8]{3,2,1,0:T(8,128)} %copy-done.12) | copy-start | bytes 98308
  411.3 53.7 %all-to-all-start.8 = ((bf16[16,4,8,2048]{3,2,1,0:T(8,128)(2,1)}), bf16[16,4,8,2048]{3,2,1,0:T(8,128)(2,1)}, u32[]{:S(2)}, u32[]{:S(2)}) async-start(bf16[16,4,8,2048]{3,2,1,0:T(8,128)(2,1)} %reshape.306), calls=%async_computation.8 | async-start | bytes 4194304 | tf_op jit(solution)/shard_map/all_to_all | solution.py:226
  418.4 29.2 %copy-start.7 = (bf16[64,8,16,128]{3,2,1,0:T(8,128)(2,1)S(1)}, bf16[64,8,16,128]{3,2,1,0:T(8,128)(2,1)}, u32[]{:S(2)}) copy-start(bf16[64,8,16,128]{3,2,1,0:T(8,128)(2,1)} %copy.291) | copy-start | bytes 6291460
  465.0 52.5 %all-to-all-start.7 = ((bf16[16,4,8,2048]{3,2,1,0:T(8,128)(2,1)}), bf16[16,4,8,2048]{3,2,1,0:T(8,128)(2,1)}, u32[]{:S(2)}, u32[]{:S(2)}) async-start(bf16[16,4,8,2048]{3,2,1,0:T(8,128)(2,1)} %reshape.303), calls=%async_computation.7 | async-start | bytes 4194304 | tf_op jit(solution)/shard_map/all_to_all | solution.py:225
  470.1 1.9 copy-start.11
  472.0 8.1 %slice-start = ((s8[8388608]{0:T(1024)(128)(4,1)}), s8[4194304]{0:T(1024)(128)(4,1)S(1)}, s32[]{:S(2)}) async-start(s8[8388608]{0:T(1024)(128)(4,1)} %bitcast.206), calls=%async_computation.9 | async-start | bytes 8388608
  472.3 7.8 %slice-start.1 = ((s8[8388608]{0:T(1024)(128)(4,1)}), s8[4194304]{0:T(1024)(128)(4,1)S(1)}, s32[]{:S(2)}) async-start(s8[8388608]{0:T(1024)(128)(4,1)} %bitcast.206), calls=%async_computation.10 | async-start | bytes 8388608
  472.3 7.8 %copy-start.19 = (bf16[256,2048]{0,1:T(8,128)(2,1)S(1)}, bf16[256,2048]{0,1:T(8,128)(2,1)}, u32[]{:S(2)}) copy-start(bf16[256,2048]{0,1:T(8,128)(2,1)} %copy.186) | copy-start | bytes 3145732
  472.3 7.8 %copy-start.27 = (bf16[1,256,2048]{1,2,0:T(8,128)(2,1)S(1)}, bf16[1,256,2048]{1,2,0:T(8,128)(2,1)}, u32[]{:S(2)}) copy-start(bf16[1,256,2048]{1,2,0:T(8,128)(2,1)} %get-tuple-element.91) | copy-start | bytes 3145732
  480.1 4.3 copy-start.21
  509.1 13.8 %copy-start.15 = (bf16[256,2048]{0,1:T(8,128)(2,1)S(1)}, bf16[256,2048]{0,1:T(8,128)(2,1)}, u32[]{:S(2)}) copy-start(bf16[256,2048]{0,1:T(8,128)(2,1)} %copy-done.14) | copy-start | bytes 3145732
  517.5 112.3 %all-to-all-start.6 = ((bf16[16,4,8,2048]{3,2,1,0:T(8,128)(2,1)}), bf16[16,4,8,2048]{3,2,1,0:T(8,128)(2,1)}, u32[]{:S(2)}, u32[]{:S(2)}) async-start(bf16[16,4,8,2048]{3,2,1,0:T(8,128)(2,1)} %reshape.300), calls=%async_computation.6 | async-start | bytes 4194304 | tf_op jit(solution)/shard_map/all_to_all | solution.py:224
  526.6 2.0 copy-start.4
  531.8 5.9 copy-start.24
  531.8 5.9 copy-start.25
  533.3 2.7 copy-start.5
  533.3 80.6 %collective-permute-start.1 = (bf16[2,256,2048]{2,1,0:T(8,128)(2,1)}, bf16[2,256,2048]{2,1,0:T(8,128)(2,1)}, u32[]{:S(2)}, u32[]{:S(2)}) collective-permute-start(bf16[2,256,2048]{2,1,0:T(8,128)(2,1)} %pad_maximum_fusion.3), channel_id=1, source_target_pairs={{2,0},{4,2},{6,4},{8,6},{10,8},{12,10},{14,12},{16,14},{18,16},{20... | collective-permute-start | bytes 6291464 | tf_op jit(solution)/shard_map/ppermute | solution.py:17
  536.1 2.9 copy-start.16
  540.8 2.4 slice-start.2
  547.0 69.0 %copy-start.8 = (f32[256,2048]{1,0:T(8,128)S(1)}, f32[256,2048]{1,0:T(8,128)}, u32[]{:S(2)}) copy-start(f32[256,2048]{1,0:T(8,128)} %copy.224) | copy-start | bytes 6291460
  618.3 2.2 copy-start.30
  631.9 3.5 copy-start.1
where the time goes:
time: 644 us; the launch traced here: 636 us
  waiting for transfers between devices  217 us (34%)
  matrix products  150 us (23%)
  local copies, waits for them, and re-layouts  104 us (16%)
  starting transfers between devices  58.5 us (9%)
  blocking collectives  55.3 us (9%)
  other arithmetic  49.6 us (8%)
    ppermute x2, waiting for transfers between devices, from_behind(): return lax.ppermute(block, axis, route)  66.9 us
    all_to_all x1, blocking collectives, body(): lax.all_to_all(grad_sent, 'seq', split_axis=0, concat_axis=0, tiled=True)  52.9 us
    unnamed x89, local copies, waits for them, and re-layouts  40.4 us
    all_to_all x1, waiting for transfers between devices, body(): lax.all_to_all(sent_key, 'seq', split_axis=0, concat_axis=0, tiled=True)  39 us
    all_to_all x1, waiting for transfers between devices, body(): lax.all_to_all(sent_query, 'seq', split_axis=0, concat_axis=0, tiled=True)  38.7 us
    all_to_all x1, waiting for transfers between devices, body(): lax.all_to_all(sent_value, 'seq', split_axis=0, concat_axis=0, tiled=True)  30.7 us
    dot_general x1, matrix products, owner_gradients(): jnp.einsum('scahd,tcbhd->hcsatb', grad_rows, val_rows, preferred_element_...  29.2 us
    all_to_all x1, waiting for transfers between devices, body(): lax.all_to_all(outputs.reshape(queries.shape), 'seq', split_axis=0, conca...  27.7 us
  transfers between devices with their start and end apart: 10, of which 7 were waited for; matrix products, arithmetic and copies ran while one was open for 37% of the time, Pallas kernels for 0%

commit v1 on v0

--- a/solution.py
+++ b/solution.py
@@ -9,6 +9,29 @@
 WINDOW = 256
 SLOTS = 128
 EPSILON = 1e-06
+
+
+def in_blocks(x, dim, size):
+    lengths = x.shape
+    parts = x.reshape(*lengths[:dim], size, lengths[dim] // size, *lengths[dim + 1 :])
+    return jnp.moveaxis(parts, dim, 0)
+
+
+def in_order(parts, dim):
+    dims = list(parts.shape[1:])
+    dims[dim] *= parts.shape[0]
+    return jnp.moveaxis(parts, 0, dim).reshape(dims)
+
+
+def pairwise_exchange(shard, axis, split_dim, concat_dim):
+    length, here = (lax.axis_size(axis), lax.axis_index(axis))
+    pieces = in_blocks(shard, split_dim, length)
+    outs = [pieces[here]]
+    for step in range(1, length):
+        sent = pieces[here ^ step]
+        outs.append(lax.ppermute(sent, axis, [(i, i ^ step) for i in range(length)]))
+    pieces = jnp.stack(outs)[here ^ jnp.arange(length)]
+    return in_order(pieces, concat_dim)
 
 
 def from_behind(block, axis, distance):
@@ -161,9 +184,7 @@
     k_five = five_dims(key_rows)
     v_five = five_dims(val_rows)
     attn_prob, weights, outputs = owner_attend(q_five, k_five, v_five, live_rows, factor)
-    returned = lax.all_to_all(
-        outputs.reshape(queries.shape), "seq", split_axis=0, concat_axis=0, tiled=True
-    )
+    returned = pairwise_exchange(outputs.reshape(queries.shape), "seq", 0, 0)
     result = (returned, q_five, k_five, v_five, attn_prob, weights, outputs)
     returned = result[0]
     attn_clu = collect(returned)

time: 644 us -> 739 us (1.15)
  waiting for transfers between devices: 217 us -> 249 us
  starting transfers between devices: 58.5 us -> 89.7 us
  local copies, waits for them, and re-layouts: 104 us -> 126 us
    ppermute x2, waiting for transfers between devices: 66.9 us -> 118 us  [from_behind(): return lax.ppermute(block, axis, route)]
    ppermute x0 -> x15, starting transfers between devices: none -> 37.2 us  [pairwise_exchange(): lax.ppermute(sent, axis, [(i, i ^ step) for i in range(length)])]
    ppermute x0 -> x15, waiting for transfers between devices: none -> 36.1 us  [pairwise_exchange(): lax.ppermute(sent, axis, [(i, i ^ step) for i in range(length)])]
    all_to_all x1 -> x0, waiting for transfers between devices: 27.7 us -> none  [body(): lax.all_to_all(outputs.reshape(queries.shape), 'seq', split_axis=0, conca...]
    all_to_all x1, waiting for transfers between devices: 30.7 us -> 15.3 us  [body(): lax.all_to_all(sent_value, 'seq', split_axis=0, concat_axis=0, tiled=True)]
    all_to_all x1 -> x0, starting transfers between devices: 10.3 us -> none  [body(): lax.all_to_all(outputs.reshape(queries.shape), 'seq', split_axis=0, conca...]
    unnamed x89 -> x93, local copies, waits for them, and re-layouts: 40.4 us -> 50.7 us
    all_to_all x1, waiting for transfers between devices: 38.7 us -> 28.5 us  [body(): lax.all_to_all(sent_query, 'seq', split_axis=0, concat_axis=0, tiled=True)]
  transfers between devices with their start and end apart: 10 -> 24, of which waited for: 7 -> 17; matrix products, arithmetic and copies ran while one was open for 37% -> 25% of each run, Pallas kernels for 0% -> 0%
where the time goes in v1:
time: 739 us; the launch traced here: 730 us
  waiting for transfers between devices  249 us (34%)
  matrix products  156 us (21%)
  local copies, waits for them, and re-layouts  126 us (17%)
  starting transfers between devices  89.7 us (12%)
  blocking collectives  57.6 us (8%)
  other arithmetic  50.8 us (7%)
    ppermute x2, waiting for transfers between devices, from_behind(): return lax.ppermute(block, axis, route)  118 us
    all_to_all x1, blocking collectives, body(): lax.all_to_all(grad_sent, 'seq', split_axis=0, concat_axis=0, tiled=True)  55.1 us
    unnamed x93, local copies, waits for them, and re-layouts  50.7 us
    all_to_all x1, waiting for transfers between devices, body(): lax.all_to_all(sent_key, 'seq', split_axis=0, concat_axis=0, tiled=True)  39 us
    ppermute x15, starting transfers between devices, pairwise_exchange(): lax.ppermute(sent, axis, [(i, i ^ step) for i in range(length)])  37.2 us
    ppermute x15, waiting for transfers between devices, pairwise_exchange(): lax.ppermute(sent, axis, [(i, i ^ step) for i in range(length)])  36.1 us
    dot_general x1, matrix products, owner_gradients(): jnp.einsum('scahd,tcbhd->hcsatb', grad_rows, val_rows, preferred_element_...  29.3 us
    all_to_all x1, waiting for transfers between devices, body(): lax.all_to_all(sent_query, 'seq', split_axis=0, concat_axis=0, tiled=True)  28.5 us
  transfers between devices with their start and end apart: 24, of which 17 were waited for; matrix products, arithmetic and copies ran while one was open for 25% of the time, Pallas kernels for 0%

profile of v1, /device:TPU:14, one launch (start us, length us, event | category | flops | bytes accessed | tf_op | source)
XLA Modules:
  0.0 730.0 jit_solution(15068404659767829096)
XLA Ops:
  5.6 7.1 all-to-all-start.1
  18.0 7.0 all-to-all-start.3
  26.6 2.7 copy.199
  29.3 4.2 reshape.294
  33.5 39.0 %all-to-all-done.3 = bf16[16,4,8,2048]{3,2,1,0:T(8,128)(2,1)S(1)} async-done(((bf16[16,4,8,2048]{3,2,1,0:T(8,128)(2,1)}), bf16[16,4,8,2048]{3,2,1,0:T(8,128)(2,1)S(1)}, u32[]{:S(2)}, u32[]{:S(2)}) %all-to-all-start.3) | async-done | bytes 2097184 | tf_op jit(solution)/shard_map/all_to_all | solution.py:180
  72.5 5.1 all-to-all-start.2
  81.4 2.9 pad_maximum_fusion
  84.3 3.8 collective-permute-start
  89.7 2.7 copy.194
  92.4 4.2 reshape.290
  96.6 28.5 %all-to-all-done.2 = bf16[16,4,8,2048]{3,2,1,0:T(8,128)(2,1)} async-done(((bf16[16,4,8,2048]{3,2,1,0:T(8,128)(2,1)}), bf16[16,4,8,2048]{3,2,1,0:T(8,128)(2,1)}, u32[]{:S(2)}, u32[]{:S(2)}) %all-to-all-start.2) | async-done | bytes 2097184 | tf_op jit(solution)/shard_map/all_to_all | solution.py:179
  125.1 9.8 %all-to-all-start = ((bf16[16,4,8,2048]{3,2,1,0:T(8,128)(2,1)}), bf16[16,4,8,2048]{3,2,1,0:T(8,128)(2,1)}, u32[]{:S(2)}, u32[]{:S(2)}) async-start(bf16[16,4,8,2048]{3,2,1,0:T(8,128)(2,1)} %reshape.290), calls=%async_computation | async-start | bytes 4194304 | tf_op jit(solution)/shard_map/all_to_all | solution.py:181
  140.2 51.4 %collective-permute-done = bf16[2,256,2048]{1,2,0:T(8,128)(2,1)} collective-permute-done((bf16[2,256,2048]{1,2,0:T(8,128)(2,1)}, bf16[2,256,2048]{1,2,0:T(8,128)(2,1)}, u32[]{:S(2)}, u32[]{:S(2)}) %collective-permute-start) | collective-permute-done | bytes 2097184 | tf_op jit(solution)/shard_map/ppermute | solution.py:40
  191.7 3.0 fusion.119
  196.9 2.8 fusion.19
  205.0 3.6 copy.291
  208.6 15.3 %all-to-all-done = bf16[16,4,8,2048]{3,2,1,0:T(8,128)(2,1)} async-done(((bf16[16,4,8,2048]{3,2,1,0:T(8,128)(2,1)}), bf16[16,4,8,2048]{3,2,1,0:T(8,128)(2,1)}, u32[]{:S(2)}, u32[]{:S(2)}) %all-to-all-start) | async-done | bytes 2097184 | tf_op jit(solution)/shard_map/all_to_all | solution.py:181
  226.2 21.0 %fusion.120 = (f32[16,4,16,8]{3,2,1,0:T(8,128)S(1)}, f32[16,4,16,8,16,8]{4,3,5,2,1,0:T(8,128)}) fusion(bf16[16,4,8,16,128,1]{4,3,2,1,0,5:T(8,128)(2,1)} %bitcast.292, bf16[16,4,8,16,128,1]{4,3,2,1,0,5:T(8,128)(2,1)} %bitcast.276, pred[16,8,16,8]{2,1,3,0:T(8,128)(4,1)S(1)} %copy-done.23, pred[16,8,16,8]{2,1,3,0:T(8,128)(4,1)S(1)} %copy-done.22, ...), kind=kOutput, calls=%fused_computation.174 | convolution fusion | flops 273670144 | bytes 8462336 | tf_op jit(solution)/shard_map/scahd,tcbhd->hcsatb/dot_general | solution.py:64
  247.1 16.0 %exponential_reduce_fusion = f32[16,4,16,8]{3,2,1,0:T(8,128)S(1)} fusion(f32[16,4,16,8,16,8]{4,3,5,2,1,0:T(8,128)} %get-tuple-element.115, f32[16,4,16,8]{3,2,1,0:T(8,128)S(1)} %get-tuple-element.114), kind=kLoop, calls=%fused_computation.3 | loop fusion | flops 2088960 | bytes 4259840 | tf_op jit(solution)/shard_map/reduce_sum | solution.py:56
  263.2 4.2 copy-done.2
  267.4 8.6 %fusion = bf16[16,4,16,8,16,8]{4,3,5,2,1,0:T(8,128)(2,1)} fusion(f32[16,4,16,8,16,8]{4,3,5,2,1,0:T(8,128)S(1)} %copy-done.2, f32[16,4,16,8]{3,2,1,0:T(8,128)S(1)} %log_add_fusion), kind=kLoop, calls=%fused_computation.5 | loop fusion | flops 2097152 | bytes 6324224 | tf_op jit(solution)/shard_map/convert_element_type | solution.py:73
  276.0 20.6 %fusion.63 = bf16[16,4,8,16,128]{4,0,2,3,1:T(8,128)(2,1)S(1)} fusion(bf16[16,4,16,8,16,8]{4,3,5,2,1,0:T(8,128)(2,1)} %fusion, bf16[16,4,8,16,128,1]{4,3,2,1,0,5:T(8,128)(2,1)S(1)} %bitcast.270), kind=kOutput, calls=%fused_computation.93 | convolution fusion | flops 269484032 | bytes 6291456 | tf_op jit(solution)/shard_map/hcsatb,tcbhd->scahd/dot_general | solution.py:75
  297.9 2.7 copy.206
  300.6 3.3 reshape_reshape.6
  305.9 7.5 %fusion.53 = (f32[256]{0:T(256)}, f32[16,128,256]{2,1,0:T(8,128)}) fusion(f32[16,512,256]{2,1,0:T(8,128)} %copy-done.3, f32[16,256]{1,0:T(8,128)S(1)} %log_add_fusion.1, pred[256,512]{0,1:T(8,128)(4,1)S(1)} %fusion.104, bf16[256,16,128]{0,2,1:T(8,128)(2,1)S(1)} %bitcast.288, bf16[256,16,128]{0,2,1:T(8,128)(2,1)S(1)} %bitcast.305), kind=kOutput, calls=%fused_computation.73 | convolution fusion | flops 551550720 | bytes 12731392 | tf_op jit(solution)/shard_map/hij,jhd->ihd/dot_general | solution.py:148
  315.3 4.0 collective-permute-start.15
  326.9 3.5 collective-permute-start.3
  331.0 3.9 collective-permute-done.3
  334.9 2.8 collective-permute-start.4
  340.9 6.5 collective-permute-start.5
  348.0 3.3 collective-permute-done.5
  353.2 4.6 collective-permute-done.6
  357.8 2.7 collective-permute-start.7
  361.2 4.8 collective-permute-done.7
  366.9 6.2 collective-permute-done.8
  373.1 3.3 collective-permute-start.9
  377.1 3.8 collective-permute-done.9
  380.9 4.2 collective-permute-start.10
  385.7 2.7 collective-permute-done.10
  388.4 4.8 collective-permute-start.11
  399.4 3.8 gather_fusion
  405.4 3.5 multiply_reduce_fusion.3
  408.9 2.9 copy.209
  411.8 2.8 multiply_reduce_fusion.1
  417.1 5.4 subtract_convert_fusion
  424.0 3.3 convert_bitcast_fusion
  427.3 3.4 copy.228
  433.0 55.1 %all_to_all.40 = bf16[16,4,8,2048]{3,2,1,0:T(8,128)(2,1)S(1)} all-to-all(bf16[16,4,8,2048]{3,2,1,0:T(8,128)(2,1)} %reshape.306), channel_id=1, replica_groups=mesh['seq'=16,'head'=2] {'seq'}, dimensions={0} | all-to-all | bytes 4194304 | tf_op jit(solution)/shard_map/all_to_all | solution.py:233
  491.1 8.1 %fusion.73 = bf16[16,4,8,16,128]{4,0,2,3,1:T(8,128)(2,1)S(1)} fusion(bf16[16,4,16,8,16,8]{4,3,5,2,1,0:T(8,128)(2,1)} %fusion, bf16[16,4,8,16,128,1]{4,3,2,1,0,5:T(8,128)(2,1)S(1)} %bitcast.267), kind=kOutput, calls=%fused_computation.95 | convolution fusion | flops 269484032 | bytes 6291456 | tf_op jit(solution)/shard_map/hcsatb,scahd->tcbhd/dot_general | solution.py:99
  499.2 2.7 copy.243
  501.9 4.2 reshape.314
  506.1 6.4 all-to-all-start.7
  512.7 29.3 %multiply_convert_fusion = bf16[16,4,16,8,16,8]{4,3,5,2,1,0:T(8,128)(2,1)} fusion(f32[16,4,16,8,16,8]{4,3,5,2,1,0:T(8,128)} %get-tuple-element.115, f32[16,4,16,8]{3,2,1,0:T(8,128)S(1)} %copy.232, f32[16,4,16,8]{3,2,1,0:T(8,128)S(1)} %log_add_fusion, bf16[16,4,8,16,128,1]{4,3,2,1,0,5:T(8,128)(2,1)} %bitcast.271, ...), kind=kOutput, calls=%fused_computation.1 | convolution fusion | flops 272629760 | bytes 10551296 | tf_op jit(solution)/shard_map/scahd,tcbhd->hcsatb/dot_general | solution.py:92
  542.0 8.1 %fusion.68 = bf16[16,4,8,16,128]{4,0,2,3,1:T(8,128)(2,1)S(1)} fusion(bf16[16,4,16,8,16,8]{4,3,5,2,1,0:T(8,128)(2,1)} %multiply_convert_fusion, bf16[16,4,8,16,128,1]{4,3,2,1,0,5:T(8,128)(2,1)S(1)} %bitcast.277), kind=kOutput, calls=%fused_computation.94 | convolution fusion | flops 270532608 | bytes 6291456 | tf_op jit(solution)/shard_map/hcsatb,scahd->tcbhd/dot_general | solution.py:98
  553.8 5.6 all-to-all-done.7
  559.4 5.1 all-to-all-start.6
  566.7 7.8 %convolution_bitcast_fusion = f32[512,16,128]{0,2,1:T(8,128)} fusion(bf16[256,16,128]{0,2,1:T(8,128)(2,1)S(1)} %bitcast.274, f32[16,512,256]{2,1,0:T(8,128)} %copy-done.3, f32[16,256]{1,0:T(8,128)S(1)} %log_add_fusion.1, pred[256,512]{0,1:T(8,128)(4,1)S(1)} %fusion.104), kind=kOutput, calls=%fused_computation.47 | convolution fusion | flops 545259520 | bytes 13778944 | tf_op jit(solution)/shard_map/hij,ihd->jhd/dot_general | solution.py:218
  574.5 6.6 multiply_convert_fusion.1
  581.1 20.9 %fusion.58 = bf16[16,4,8,16,128]{4,0,2,3,1:T(8,128)(2,1)S(1)} fusion(bf16[16,4,16,8,16,8]{4,3,5,2,1,0:T(8,128)(2,1)} %multiply_convert_fusion, bf16[16,4,8,16,128,1]{4,3,2,1,0,5:T(8,128)(2,1)S(1)} %bitcast.293), kind=kOutput, calls=%fused_computation.92 | convolution fusion | flops 270532608 | bytes 6291456 | tf_op jit(solution)/shard_map/hcsatb,tcbhd->scahd/dot_general | solution.py:97
  605.6 6.2 all-to-all-done.6
  611.9 5.4 all-to-all-start.5
  617.3 3.7 convolution_bitcast_fusion.1
  627.7 2.7 collective-permute-start.16
  641.4 66.9 %collective-permute-done.16 = bf16[2,256,2048]{2,1,0:T(8,128)(2,1)} collective-permute-done((bf16[2,256,2048]{2,1,0:T(8,128)(2,1)}, bf16[2,256,2048]{2,1,0:T(8,128)(2,1)}, u32[]{:S(2)}, u32[]{:S(2)}) %collective-permute-start.16) | collective-permute-done | bytes 2097184 | tf_op jit(solution)/shard_map/ppermute | solution.py:40
  (168 shorter events, 120.8 us)
Async XLA Ops:
  0.6 12.1 %copy-start = (bf16[256,2048]{1,0:T(8,128)(2,1)S(1)}, bf16[256,2048]{1,0:T(8,128)(2,1)}, u32[]{:S(2)}) copy-start(bf16[256,2048]{1,0:T(8,128)(2,1)} %param.23) | copy-start | bytes 3145732
  3.6 84.6 %copy-start.24 = (s32[16,256]{1,0:T(8,128)}, s32[16,256]{1,0:T(8,128)S(1)}, u32[]{:S(2)}) copy-start(s32[16,256]{1,0:T(8,128)S(1)} %multiply_add_fusion) | copy-start | bytes 49156
  5.6 12.4 %all-to-all-start.1 = ((bf16[16,2,256]{2,1,0:T(2,128)(2,1)}), bf16[16,2,256]{2,1,0:T(2,128)(2,1)S(1)}, u32[]{:S(2)}, u32[]{:S(2)}) async-start(bf16[16,2,256]{2,1,0:T(2,128)(2,1)} %reshape.342), calls=%async_computation.1 | async-start | bytes 32768 | tf_op jit(solution)/shard_map/all_to_all | solution.py:182
  18.0 7.1 copy-start.30
  18.0 54.5 %all-to-all-start.3 = ((bf16[16,4,8,2048]{3,2,1,0:T(8,128)(2,1)}), bf16[16,4,8,2048]{3,2,1,0:T(8,128)(2,1)S(1)}, u32[]{:S(2)}, u32[]{:S(2)}) async-start(bf16[16,4,8,2048]{3,2,1,0:T(8,128)(2,1)} %reshape.297), calls=%async_computation.3 | async-start | bytes 4194304 | tf_op jit(solution)/shard_map/all_to_all | solution.py:180
  72.5 52.6 %all-to-all-start.2 = ((bf16[16,4,8,2048]{3,2,1,0:T(8,128)(2,1)}), bf16[16,4,8,2048]{3,2,1,0:T(8,128)(2,1)}, u32[]{:S(2)}, u32[]{:S(2)}) async-start(bf16[16,4,8,2048]{3,2,1,0:T(8,128)(2,1)} %reshape.294), calls=%async_computation.2 | async-start | bytes 4194304 | tf_op jit(solution)/shard_map/all_to_all | solution.py:179
  81.4 6.7 copy-start.31
  84.3 107.4 %collective-permute-start = (bf16[2,256,2048]{1,2,0:T(8,128)(2,1)}, bf16[2,256,2048]{1,2,0:T(8,128)(2,1)}, u32[]{:S(2)}, u32[]{:S(2)}) collective-permute-start(bf16[2,256,2048]{1,2,0:T(8,128)(2,1)} %pad_maximum_fusion), channel_id=1, source_target_pairs={{0,2},{2,4},{4,6},{6,8},{8,10},{10,12},{12,14},{14,16},{16,18},{18... | collective-permute-start | bytes 6291464 | tf_op jit(solution)/shard_map/ppermute | solution.py:40
  125.1 98.7 %all-to-all-start = ((bf16[16,4,8,2048]{3,2,1,0:T(8,128)(2,1)}), bf16[16,4,8,2048]{3,2,1,0:T(8,128)(2,1)}, u32[]{:S(2)}, u32[]{:S(2)}) async-start(bf16[16,4,8,2048]{3,2,1,0:T(8,128)(2,1)} %reshape.290), calls=%async_computation | async-start | bytes 4194304 | tf_op jit(solution)/shard_map/all_to_all | solution.py:181
  137.7 59.2 %copy-start.12 = (bf16[256,2048]{0,1:T(8,128)(2,1)}, bf16[256,2048]{0,1:T(8,128)(2,1)S(1)}, u32[]{:S(2)}) copy-start(bf16[256,2048]{0,1:T(8,128)(2,1)S(1)} %copy.286) | copy-start | bytes 3145732
  199.7 3.3 copy-start.3
  223.9 2.3 copy-start.22
  223.9 2.3 copy-start.23
  226.1 49.8 %copy-start.6 = (bf16[64,8,16,128]{3,2,1,0:T(8,128)(2,1)}, bf16[64,8,16,128]{3,2,1,0:T(8,128)(2,1)S(1)}, u32[]{:S(2)}) copy-start(bf16[64,8,16,128]{3,2,1,0:T(8,128)(2,1)S(1)} %copy.290) | copy-start | bytes 6291460
  247.1 20.2 %copy-start.2 = (f32[16,4,16,8,16,8]{4,3,5,2,1,0:T(8,128)S(1)}, f32[16,4,16,8,16,8]{4,3,5,2,1,0:T(8,128)}, u32[]{:S(2)}) copy-start(f32[16,4,16,8,16,8]{4,3,5,2,1,0:T(8,128)} %get-tuple-element.115) | copy-start | bytes 12582916
  296.5 1.4 copy-start.9
  303.9 1.7 copy-start.15
  303.9 2.0 copy-start.20
  305.0 16.7 %collective-permute-start.1 = (bf16[1,4,8,2048]{3,2,1,0:T(8,128)(2,1)}, bf16[1,4,8,2048]{3,2,1,0:T(8,128)(2,1)}, u32[]{:S(2)}, u32[]{:S(2)}) collective-permute-start(bf16[1,4,8,2048]{3,2,1,0:T(8,128)(2,1)} %get-tuple-element.104), channel_id=1, source_target_pairs={{0,2},{2,0},{4,6},{6,4},{8,10},{10,8},{12,14},{14,12},{16,18},{18,... | collective-permute-start | bytes 393224 | tf_op jit(solution)/shard_map/ppermute | solution.py:32
  315.3 83.4 %collective-permute-start.15 = (bf16[1,4,8,2048]{3,2,1,0:T(8,128)(2,1)S(1)}, bf16[1,4,8,2048]{3,2,1,0:T(8,128)(2,1)S(1)}, u32[]{:S(2)}, u32[]{:S(2)}) collective-permute-start(bf16[1,4,8,2048]{3,2,1,0:T(8,128)(2,1)S(1)} %get-tuple-element.90), channel_id=1, source_target_pairs={{0,30},{2,28},{4,26},{6,24},{8,22},{10,20},{12,18},{14,16},{16,14}... | collective-permute-start | bytes 393224 | tf_op jit(solution)/shard_map/ppermute | solution.py:32
  319.4 78.7 %collective-permute-start.14 = (bf16[1,4,8,2048]{3,2,1,0:T(8,128)(2,1)S(1)}, bf16[1,4,8,2048]{3,2,1,0:T(8,128)(2,1)S(1)}, u32[]{:S(2)}, u32[]{:S(2)}) collective-permute-start(bf16[1,4,8,2048]{3,2,1,0:T(8,128)(2,1)S(1)} %get-tuple-element.91), channel_id=1, source_target_pairs={{0,28},{2,30},{4,24},{6,26},{8,20},{10,22},{12,16},{14,18},{16,12}... | collective-permute-start | bytes 393224 | tf_op jit(solution)/shard_map/ppermute | solution.py:32
  319.4 78.1 %collective-permute-start.13 = (bf16[1,4,8,2048]{3,2,1,0:T(8,128)(2,1)S(1)}, bf16[1,4,8,2048]{3,2,1,0:T(8,128)(2,1)S(1)}, u32[]{:S(2)}, u32[]{:S(2)}) collective-permute-start(bf16[1,4,8,2048]{3,2,1,0:T(8,128)(2,1)S(1)} %get-tuple-element.92), channel_id=1, source_target_pairs={{0,26},{2,24},{4,30},{6,28},{8,18},{10,16},{12,22},{14,20},{16,10}... | collective-permute-start | bytes 393224 | tf_op jit(solution)/shard_map/ppermute | solution.py:32
  319.4 77.4 %collective-permute-start.12 = (bf16[1,4,8,2048]{3,2,1,0:T(8,128)(2,1)S(1)}, bf16[1,4,8,2048]{3,2,1,0:T(8,128)(2,1)S(1)}, u32[]{:S(2)}, u32[]{:S(2)}) collective-permute-start(bf16[1,4,8,2048]{3,2,1,0:T(8,128)(2,1)S(1)} %get-tuple-element.93), channel_id=1, source_target_pairs={{0,24},{2,26},{4,28},{6,30},{8,16},{10,18},{12,20},{14,22},{16,8},... | collective-permute-start | bytes 393224 | tf_op jit(solution)/shard_map/ppermute | solution.py:32
  321.7 5.2 collective-permute-start.2
  326.9 8.0 %collective-permute-start.3 = (bf16[1,4,8,2048]{3,2,1,0:T(8,128)(2,1)}, bf16[1,4,8,2048]{3,2,1,0:T(8,128)(2,1)S(1)}, u32[]{:S(2)}, u32[]{:S(2)}) collective-permute-start(bf16[1,4,8,2048]{3,2,1,0:T(8,128)(2,1)} %get-tuple-element.102), channel_id=1, source_target_pairs={{0,6},{2,4},{4,2},{6,0},{8,14},{10,12},{12,10},{14,8},{16,22},{18,... | collective-permute-start | bytes 393224 | tf_op jit(solution)/shard_map/ppermute | solution.py:32
  334.9 6.0 collective-permute-start.4
  340.9 10.4 %collective-permute-start.5 = (bf16[1,4,8,2048]{3,2,1,0:T(8,128)(2,1)}, bf16[1,4,8,2048]{3,2,1,0:T(8,128)(2,1)S(1)}, u32[]{:S(2)}, u32[]{:S(2)}) collective-permute-start(bf16[1,4,8,2048]{3,2,1,0:T(8,128)(2,1)} %get-tuple-element.100), channel_id=1, source_target_pairs={{0,10},{2,8},{4,14},{6,12},{8,2},{10,0},{12,6},{14,4},{16,26},{18,... | collective-permute-start | bytes 393224 | tf_op jit(solution)/shard_map/ppermute | solution.py:32
  351.3 6.6 collective-permute-start.6
  357.8 8.2 %collective-permute-start.7 = (bf16[1,4,8,2048]{3,2,1,0:T(8,128)(2,1)}, bf16[1,4,8,2048]{3,2,1,0:T(8,128)(2,1)S(1)}, u32[]{:S(2)}, u32[]{:S(2)}) collective-permute-start(bf16[1,4,8,2048]{3,2,1,0:T(8,128)(2,1)} %get-tuple-element.98), channel_id=1, source_target_pairs={{0,14},{2,12},{4,10},{6,8},{8,6},{10,4},{12,2},{14,0},{16,30},{18,... | collective-permute-start | bytes 393224 | tf_op jit(solution)/shard_map/ppermute | solution.py:32
  366.0 7.1 collective-permute-start.8
  373.1 7.8 %collective-permute-start.9 = (bf16[1,4,8,2048]{3,2,1,0:T(8,128)(2,1)}, bf16[1,4,8,2048]{3,2,1,0:T(8,128)(2,1)S(1)}, u32[]{:S(2)}, u32[]{:S(2)}) collective-permute-start(bf16[1,4,8,2048]{3,2,1,0:T(8,128)(2,1)} %get-tuple-element.96), channel_id=1, source_target_pairs={{0,18},{2,16},{4,22},{6,20},{8,26},{10,24},{12,30},{14,28},{16,2},... | collective-permute-start | bytes 393224 | tf_op jit(solution)/shard_map/ppermute | solution.py:32
  380.9 7.5 %collective-permute-start.10 = (bf16[1,4,8,2048]{3,2,1,0:T(8,128)(2,1)S(1)}, bf16[1,4,8,2048]{3,2,1,0:T(8,128)(2,1)S(1)}, u32[]{:S(2)}, u32[]{:S(2)}) collective-permute-start(bf16[1,4,8,2048]{3,2,1,0:T(8,128)(2,1)S(1)} %get-tuple-element.95), channel_id=1, source_target_pairs={{0,20},{2,22},{4,16},{6,18},{8,28},{10,30},{12,24},{14,26},{16,4},... | collective-permute-start | bytes 393224 | tf_op jit(solution)/shard_map/ppermute | solution.py:32
  388.4 7.7 %collective-permute-start.11 = (bf16[1,4,8,2048]{3,2,1,0:T(8,128)(2,1)S(1)}, bf16[1,4,8,2048]{3,2,1,0:T(8,128)(2,1)S(1)}, u32[]{:S(2)}, u32[]{:S(2)}) collective-permute-start(bf16[1,4,8,2048]{3,2,1,0:T(8,128)(2,1)S(1)} %get-tuple-element.94), channel_id=1, source_target_pairs={{0,22},{2,20},{4,18},{6,16},{8,30},{10,28},{12,26},{14,24},{16,6},... | collective-permute-start | bytes 393224 | tf_op jit(solution)/shard_map/ppermute | solution.py:32
  403.2 2.2 copy-start.25
  408.9 2.9 copy-start.29
  408.9 2.9 copy-start.27
  408.9 3.0 copy-start.28
  488.1 1.6 copy-start.10
  506.1 53.3 %all-to-all-start.7 = ((bf16[16,4,8,2048]{3,2,1,0:T(8,128)(2,1)}), bf16[16,4,8,2048]{3,2,1,0:T(8,128)(2,1)}, u32[]{:S(2)}, u32[]{:S(2)}) async-start(bf16[16,4,8,2048]{3,2,1,0:T(8,128)(2,1)} %reshape.314), calls=%async_computation.7 | async-start | bytes 4194304 | tf_op jit(solution)/shard_map/all_to_all | solution.py:247
  512.7 29.3 %copy-start.7 = (bf16[64,8,16,128]{3,2,1,0:T(8,128)(2,1)S(1)}, bf16[64,8,16,128]{3,2,1,0:T(8,128)(2,1)}, u32[]{:S(2)}) copy-start(bf16[64,8,16,128]{3,2,1,0:T(8,128)(2,1)} %copy.291) | copy-start | bytes 6291460
  559.4 52.5 %all-to-all-start.6 = ((bf16[16,4,8,2048]{3,2,1,0:T(8,128)(2,1)}), bf16[16,4,8,2048]{3,2,1,0:T(8,128)(2,1)}, u32[]{:S(2)}, u32[]{:S(2)}) async-start(bf16[16,4,8,2048]{3,2,1,0:T(8,128)(2,1)} %reshape.311), calls=%async_computation.6 | async-start | bytes 4194304 | tf_op jit(solution)/shard_map/all_to_all | solution.py:246
  564.5 1.9 copy-start.11
  566.7 7.8 %copy-start.16 = (bf16[256,2048]{0,1:T(8,128)(2,1)S(1)}, bf16[256,2048]{0,1:T(8,128)(2,1)}, u32[]{:S(2)}) copy-start(bf16[256,2048]{0,1:T(8,128)(2,1)} %copy.186) | copy-start | bytes 3145732
  566.7 7.8 %copy-start.21 = (bf16[1,256,2048]{1,2,0:T(8,128)(2,1)S(1)}, bf16[1,256,2048]{1,2,0:T(8,128)(2,1)}, u32[]{:S(2)}) copy-start(bf16[1,256,2048]{1,2,0:T(8,128)(2,1)} %get-tuple-element.107) | copy-start | bytes 3145732
  574.5 6.6 copy-start.17
  605.6 11.7 %copy-start.13 = (bf16[256,2048]{0,1:T(8,128)(2,1)S(1)}, bf16[256,2048]{0,1:T(8,128)(2,1)}, u32[]{:S(2)}) copy-start(bf16[256,2048]{0,1:T(8,128)(2,1)} %copy-done.12) | copy-start | bytes 3145732
  611.9 112.3 %all-to-all-start.5 = ((bf16[16,4,8,2048]{3,2,1,0:T(8,128)(2,1)}), bf16[16,4,8,2048]{3,2,1,0:T(8,128)(2,1)}, u32[]{:S(2)}, u32[]{:S(2)}) async-start(bf16[16,4,8,2048]{3,2,1,0:T(8,128)(2,1)} %reshape.308), calls=%async_computation.5 | async-start | bytes 4194304 | tf_op jit(solution)/shard_map/all_to_all | solution.py:245
  621.0 2.0 copy-start.4
  626.2 5.9 copy-start.18
  626.2 5.9 copy-start.19
  627.7 2.7 copy-start.5
  627.7 80.7 %collective-permute-start.16 = (bf16[2,256,2048]{2,1,0:T(8,128)(2,1)}, bf16[2,256,2048]{2,1,0:T(8,128)(2,1)}, u32[]{:S(2)}, u32[]{:S(2)}) collective-permute-start(bf16[2,256,2048]{2,1,0:T(8,128)(2,1)} %pad_maximum_fusion.3), channel_id=1, source_target_pairs={{2,0},{4,2},{6,4},{8,6},{10,8},{12,10},{14,12},{16,14},{18,16},{20... | collective-permute-start | bytes 6291464 | tf_op jit(solution)/shard_map/ppermute | solution.py:40
  630.4 2.9 copy-start.14
  635.2 2.4 slice-start
  641.4 69.0 %copy-start.8 = (f32[256,2048]{1,0:T(8,128)S(1)}, f32[256,2048]{1,0:T(8,128)}, u32[]{:S(2)}) copy-start(f32[256,2048]{1,0:T(8,128)} %copy.224) | copy-start | bytes 6291460
  712.7 2.2 copy-start.26
  726.3 3.5 copy-start.1
